TPU v7x, 32 devices: a whole 2x2x4 slice. The times are simulated.
32 devices in a mesh: seq: 8 (over y, x, core), ch: 4 (over z).
Axes of the slice: x: 2, y: 2, z: 4, core: 2. Of those that a mesh axis runs over, the one named last changes fastest.
Arguments:
- inputs: bfloat16 [1536, 131072], P('ch', 'seq'), may hold values from -6 to 6
- gating: bfloat16 [1536, 131072], P('ch', 'seq'), may hold values from -6 to 6
- upstream: bfloat16 [1536, 131072], P('ch', 'seq'), may hold values from -6 to 6
- factor_one: bfloat16 [512, 512], replicated, may hold values from -0.25 to 0.25
- factor_two: bfloat16 [256, 256], replicated, may hold values from -0.375 to 0.375
- factor_three: bfloat16 [256, 256], replicated, may hold values from -0.375 to 0.375
- factor_four: bfloat16 [512, 512], replicated, may hold values from -0.25 to 0.25
- kernel_cols: float32 [1536, 512], P('ch'), may hold values from -4 to 4
- kernel_rows: float32 [1536, 256], P('ch'), may hold values from -4 to 4
Outputs:
- input_grad: bfloat16 [1536, 131072], P('ch', 'seq')
- gating_grad: bfloat16 [1536, 131072], P('ch', 'seq')
- one_grad: float32 [512, 512], replicated
- two_grad: float32 [256, 256], replicated
- three_grad: float32 [256, 256], replicated
- four_grad: float32 [512, 512], replicated
- cols_grad: float32 [1536, 512], P('ch')
- rows_grad: float32 [1536, 256], P('ch')
All inputs are finite; a program needn't handle non-finite values.
Results may differ from a plain program's by a relative error of at most 0.0076.
Values may be sent and summed in bfloat16 or wider, within the bound.
A program may use at most 384 MiB of HBM per device.

v0:
```python
import math
import jax
import jax.numpy as jnp
from jax import lax
from jax.sharding import PartitionSpec as P

P1 = 256
P2 = 512
C = 1536


def local(
    inputs,
    gating,
    upstream,
    factor_one,
    factor_two,
    factor_three,
    factor_four,
    kernel_cols,
    kernel_rows,
):
    width = inputs.shape[0]
    length = inputs.shape[1]
    parts = lax.axis_size("seq")
    flt = jnp.float32
    half = jnp.bfloat16
    rows_local = length // P2
    up_gate = (upstream.astype(flt) * gating.astype(flt)).astype(half)
    moved_in, moved_gate = (
        lax.all_to_all(inputs, "seq", split_axis=0, concat_axis=1, tiled=True),
        lax.all_to_all(up_gate, "seq", split_axis=0, concat_axis=1, tiled=True),
    )
    several = width // parts
    offset = lax.axis_index("seq") * several
    local_cols = lax.dynamic_slice_in_dim(kernel_cols, offset, several, 0)
    local_rows = lax.dynamic_slice_in_dim(kernel_rows, offset, several, 0)
    shaped = moved_in.reshape(several, P1, P2)
    gate_rows = moved_gate.reshape(several, P1, P2)
    first_prod = jnp.einsum("cij,jk->cik", shaped, factor_one, preferred_element_type=flt)
    first_out = (first_prod * local_cols[:, None, :]).astype(half)
    left_prod = jnp.einsum("ki,cij->ckj", factor_two, first_out, preferred_element_type=flt)
    left_out = (left_prod * local_rows[:, :, None]).astype(half)
    second = jnp.einsum("ki,cij->ckj", factor_three, left_out, preferred_element_type=flt).astype(
        half
    )
    grad_four = jnp.einsum("cij,cik->jk", second, gate_rows, preferred_element_type=flt)
    grad_second = jnp.einsum(
        "cik,jk->cij", gate_rows, factor_four, preferred_element_type=flt
    ).astype(half)
    grad_three = jnp.einsum("ckj,cij->ki", grad_second, left_out, preferred_element_type=flt)
    grad_left = jnp.einsum("ki,ckj->cij", factor_three, grad_second, preferred_element_type=flt)
    rows_part = jnp.sum(grad_left * left_prod, axis=2)
    grad_prod = (grad_left * local_rows[:, :, None]).astype(half)
    grad_two = jnp.einsum("ckj,cij->ki", grad_prod, first_out, preferred_element_type=flt)
    grad_first = jnp.einsum(
        "ki,ckj->cij", factor_two, grad_prod, preferred_element_type=flt
    ).astype(half)
    cols_part = jnp.sum(grad_first.astype(flt) * first_prod, axis=1)
    grad_inner = (grad_first.astype(flt) * local_cols[:, None, :]).astype(half)
    grad_one = jnp.einsum("cij,cik->jk", shaped, grad_inner, preferred_element_type=flt)
    local_input = jnp.einsum(
        "cik,jk->cij", grad_inner, factor_one, preferred_element_type=flt
    ).astype(half)
    input_grad, second_rows = (
        lax.all_to_all(
            local_input.reshape(several, P1 * P2), "seq", split_axis=1, concat_axis=0, tiled=True
        ),
        lax.all_to_all(
            second.reshape(several, P1 * P2), "seq", split_axis=1, concat_axis=0, tiled=True
        ),
    )
    cols_sum, rows_sum = (
        lax.all_gather(cols_part, "seq", axis=0, tiled=True),
        lax.all_gather(rows_part, "seq", axis=0, tiled=True),
    )
    final_prod = jnp.einsum(
        "cij,jk->cik",
        second_rows.reshape(width, rows_local, P2),
        factor_four,
        preferred_element_type=flt,
    )
    gating_grad = (
        (upstream.reshape(width, rows_local, P2).astype(flt) * final_prod)
        .astype(half)
        .reshape(width, length)
    )
    one_sum, two_sum, three_sum, four_sum = lax.psum(
        (grad_one, grad_two, grad_three, grad_four), ("seq", "ch")
    )
    scale_one = 1.0 / math.sqrt(P1 * C)
    scale_two = 1.0 / math.sqrt(P2 * C)
    return (
        input_grad,
        gating_grad,
        one_sum * scale_one,
        two_sum * scale_two,
        three_sum * scale_two,
        four_sum * scale_one,
        cols_sum / math.sqrt(P1),
        rows_sum / math.sqrt(P2),
    )


def solution(mesh):
    in_specs = (
        P("ch", "seq"),
        P("ch", "seq"),
        P("ch", "seq"),
        P(),
        P(),
        P(),
        P(),
        P("ch", None),
        P("ch", None),
    )
    out_specs = (P("ch", "seq"), P("ch", "seq"), P(), P(), P(), P(), P("ch", None), P("ch", None))
    return jax.shard_map(local, mesh=mesh, in_specs=in_specs, out_specs=out_specs, check_vma=False)
```

profile of v0, /device:TPU:0, one launch (start us, length us, event | category | flops | bytes accessed | tf_op | source)
XLA Modules:
  0.0 879.9 jit_solution(3477879930901490185)
XLA Ops:
  17.1 144.0 %all_to_all.67 = bf16[8,48,16384]{2,1,0:T(8,128)(2,1)} all-to-all(bf16[8,48,16384]{2,1,0:T(8,128)(2,1)S(1)} %bitcast.84), channel_id=1, replica_groups=mesh['seq'=8,'ch'=4] {'seq'}, dimensions={0} | all-to-all | bytes 25165824 | tf_op jit(solution)/shard_map/all_to_all | solution.py:32
  167.3 14.4 %copy.71 = bf16[48,8,16384]{2,1,0:T(8,128)(2,1)} copy(bf16[48,8,16384]{2,0,1:T(8,128)(2,1)} %bitcast.82) | data formatting | bytes 25165824 | tf_op jit(solution)/shard_map/all_to_all | solution.py:32
  181.7 19.5 %reshape.52 = bf16[48,256,512]{2,1,0:T(8,128)(2,1)} reshape(bf16[48,8,16384]{2,1,0:T(8,128)(2,1)} %copy.71) | data formatting | bytes 25165824 | tf_op jit(solution)/shard_map/reshape | solution.py:39
  201.3 11.6 %convolution_convert_fusion.1 = bf16[48,256,512]{2,1,0:T(8,128)(2,1)S(1)} fusion(bf16[48,256,512]{2,1,0:T(8,128)(2,1)} %reshape.52, bf16[512,512]{1,0:T(8,128)(2,1)S(1)} %copy-done.4), kind=kOutput, calls=%fused_computation.19 | convolution fusion | flops 6448742400 | bytes 25690112 | tf_op jit(solution)/shard_map/cik,jk->cij/dot_general | solution.py:48
  217.4 10.1 %fusion.39 = f32[48,512,256]{2,1,0:T(8,128)} fusion(bf16[48,256,512]{2,1,0:T(8,128)(2,1)S(1)} %convolution_convert_fusion.1, bf16[256,256]{1,0:T(8,128)(2,1)S(1)} %copy-done.7), kind=kOutput, calls=%fused_computation.39 | convolution fusion | flops 3221225472 | bytes 37879808 | tf_op jit(solution)/shard_map/ki,ckj->cij/dot_general | solution.py:52
  227.5 14.8 %convolution_convert_fusion = bf16[48,512,256]{1,2,0:T(8,128)(2,1)} fusion(f32[48,512,256]{2,1,0:T(8,128)} %fusion.39, f32[48,256]{1,0:T(8,128)S(1)} %constant_dynamic-slice_fusion.1, bf16[256,256]{1,0:T(8,128)(2,1)S(1)} %copy-done.6), kind=kOutput, calls=%fused_computation.17 | convolution fusion | flops 3240099840 | bytes 37928960 | tf_op jit(solution)/shard_map/ki,ckj->cij/dot_general | solution.py:56
  242.3 14.4 %fusion.10 = bf16[48,256,512]{2,1,0:T(8,128)(2,1)} fusion(bf16[48,512,256]{1,2,0:T(8,128)(2,1)} %convolution_convert_fusion, f32[48,512]{1,0:T(8,128)S(1)} %constant_dynamic-slice_fusion, bf16[512,512]{1,0:T(8,128)(2,1)S(1)} %copy-done.3), kind=kOutput, calls=%fused_computation.18 | convolution fusion | flops 6467616768 | bytes 25788416 | tf_op jit(solution)/shard_map/cik,jk->cij/dot_general | solution.py:62
  256.7 19.8 %all_to_all.53 = bf16[48,8,16384]{2,1,0:T(8,128)(2,1)} reshape(bf16[48,256,512]{2,1,0:T(8,128)(2,1)} %fusion.10) | data formatting | bytes 25165824 | tf_op jit(solution)/shard_map/all_to_all | solution.py:66
  276.5 14.5 %copy.75 = bf16[48,8,16384]{2,0,1:T(8,128)(2,1)} copy(bf16[48,8,16384]{2,1,0:T(8,128)(2,1)} %all_to_all.53) | data formatting | bytes 25165824 | tf_op jit(solution)/shard_map/all_to_all | solution.py:66
  291.0 14.5 %all-to-all-done.2 = bf16[8,48,16384]{2,1,0:T(8,128)(2,1)} async-done(((bf16[8,48,16384]{2,1,0:T(8,128)(2,1)}), bf16[8,48,16384]{2,1,0:T(8,128)(2,1)}, u32[]{:S(2)}, u32[]{:S(2)}) %all-to-all-start.2) | async-done | bytes 12582944 | tf_op jit(solution)/shard_map/all_to_all | solution.py:31
  310.8 17.6 %copy.76 = f32[384,16384]{0,1:T(8,128)} copy(bf16[384,16384]{1,0:T(8,128)(2,1)} %param.11) | data formatting | bytes 37748736 | tf_op jit(solution)/shard_map/convert_element_type | solution.py:29
  328.4 24.6 %copy.82 = f32[384,32,512]{2,0,1:T(8,128)} copy(f32[384,32,512]{0,2,1:T(8,128)} %bitcast.80) | data formatting | bytes 50331648 | tf_op jit(solution)/shard_map/convert_element_type | solution.py:84
  353.0 14.4 %copy.77 = bf16[48,8,16384]{2,1,0:T(8,128)(2,1)} copy(bf16[48,8,16384]{2,0,1:T(8,128)(2,1)} %bitcast.12) | data formatting | bytes 25165824 | tf_op jit(solution)/shard_map/all_to_all | solution.py:31
  367.4 19.5 %reshape.53 = bf16[48,256,512]{2,1,0:T(8,128)(2,1)} reshape(bf16[48,8,16384]{2,1,0:T(8,128)(2,1)} %copy.77) | data formatting | bytes 25165824 | tf_op jit(solution)/shard_map/reshape | solution.py:38
  387.0 18.9 %fusion.1 = (f32[48,512]{1,0:T(8,128)}, f32[48,256,512]{2,1,0:T(8,128)}) fusion(bf16[48,512,256]{1,2,0:T(8,128)(2,1)} %convolution_convert_fusion, bf16[48,256,512]{2,1,0:T(8,128)(2,1)} %reshape.53, bf16[512,512]{1,0:T(8,128)(2,1)S(1)} %copy-done.3), kind=kOutput, calls=%fused_computation.3 | convolution fusion | flops 6461300736 | bytes 50954240 | tf_op jit(solution)/shard_map/cij,jk->cik/dot_general | solution.py:40
  405.9 16.3 %fusion.21 = f32[48,512,256]{2,1,0:T(8,128)} fusion(f32[48,256,512]{2,1,0:T(8,128)} %get-tuple-element.45, f32[48,512]{1,0:T(8,128)S(1)} %constant_dynamic-slice_fusion, bf16[256,256]{1,0:T(8,128)(2,1)S(1)} %copy-done.6), kind=kOutput, calls=%fused_computation.22 | convolution fusion | flops 3233808384 | bytes 50561024 | tf_op jit(solution)/shard_map/ki,cij->ckj/dot_general | solution.py:42
  422.2 14.5 %convert_bitcast_fusion = bf16[48,256,512]{1,2,0:T(8,128)(2,1)} fusion(f32[48,512,256]{2,1,0:T(8,128)} %fusion.21, f32[48,256]{1,0:T(8,128)S(1)} %constant_dynamic-slice_fusion.1, bf16[256,256]{1,0:T(8,128)(2,1)S(1)} %copy-done.7), kind=kOutput, calls=%fused_computation.14 | convolution fusion | flops 3240099840 | bytes 37928960 | tf_op jit(solution)/shard_map/ki,cij->ckj/dot_general | solution.py:44
  436.7 16.7 %copy.79 = bf16[48,256,512]{2,1,0:T(8,128)(2,1)} copy(bf16[48,256,512]{1,2,0:T(8,128)(2,1)} %convert_bitcast_fusion) | data formatting | bytes 25165824 | tf_op jit(solution)/shard_map/convert_element_type | solution.py:44
  453.4 19.5 %all_to_all.60 = bf16[48,8,16384]{2,1,0:T(8,128)(2,1)} reshape(bf16[48,256,512]{2,1,0:T(8,128)(2,1)} %copy.79) | data formatting | bytes 25165824 | tf_op jit(solution)/shard_map/all_to_all | solution.py:69
  472.9 26.0 %copy.80 = bf16[48,8,16384]{2,0,1:T(8,128)(2,1)} copy(bf16[48,8,16384]{2,1,0:T(8,128)(2,1)} %all_to_all.60) | data formatting | bytes 25165824 | tf_op jit(solution)/shard_map/all_to_all | solution.py:69
  499.0 16.0 %fusion.28 = f32[256,256]{1,0:T(8,128)} fusion(bf16[48,256,512]{2,1,0:T(8,128)(2,1)} %copy-done.2, f32[48,512,256]{2,1,0:T(8,128)} %fusion.21, f32[48,256]{1,0:T(8,128)S(1)} %constant_dynamic-slice_fusion.1), kind=kOutput, calls=%fused_computation.26 | convolution fusion | flops 3233808384 | bytes 38060032 | tf_op jit(solution)/shard_map/ckj,cij->ki/dot_general | solution.py:51
  520.3 14.1 %fusion.22 = f32[512,512]{0,1:T(8,128)} fusion(bf16[48,256,512]{2,1,0:T(8,128)(2,1)} %reshape.53, bf16[48,512,256]{1,2,0:T(8,128)(2,1)} %convolution_convert_fusion, f32[48,512]{1,0:T(8,128)S(1)} %constant_dynamic-slice_fusion), kind=kOutput, calls=%fused_computation.23 | convolution fusion | flops 6461325312 | bytes 26312704 | tf_op jit(solution)/shard_map/cij,cik->jk/dot_general | solution.py:61
  534.4 12.6 %convolution_bitcast_fusion = f32[512,512]{0,1:T(8,128)} fusion(bf16[48,256,512]{1,2,0:T(8,128)(2,1)} %convert_bitcast_fusion, bf16[48,256,512]{2,1,0:T(8,128)(2,1)} %reshape.52), kind=kOutput, calls=%fused_computation.24 | convolution fusion | flops 6442450944 | bytes 26214400 | tf_op jit(solution)/shard_map/cij,cik->jk/dot_general | solution.py:47
  547.0 17.6 %fusion.25 = f32[256,256]{1,0:T(8,128)} fusion(f32[48,256,512]{2,1,0:T(8,128)} %get-tuple-element.45, f32[48,512]{1,0:T(8,128)S(1)} %constant_dynamic-slice_fusion, f32[48,512,256]{2,1,0:T(8,128)} %fusion.39, f32[48,256]{1,0:T(8,128)S(1)} %constant_dynamic-slice_fusion.1), kind=kOutput, calls=%fused_computation.25 | convolution fusion | flops 3246391296 | bytes 50741248 | tf_op jit(solution)/shard_map/ckj,cij->ki/dot_general | solution.py:55
  564.6 16.7 %multiply_reduce_fusion = f32[48,256]{1,0:T(8,128)S(1)} fusion(f32[48,512,256]{2,1,0:T(8,128)} %fusion.39, f32[48,512,256]{2,1,0:T(8,128)} %fusion.21), kind=kLoop, calls=%fused_computation.4 | loop fusion | flops 12570624 | bytes 50380800 | tf_op jit(solution)/shard_map/reduce_sum | solution.py:53
  581.3 89.7 %all_gather.7 = f32[384,256]{1,0:T(8,128)S(1)} all-gather(f32[48,256]{1,0:T(8,128)S(1)} %multiply_reduce_fusion), channel_id=1, replica_groups=mesh['seq'=8,'ch'=4] {'seq'}, dimensions={0}, use_global_device_ids=true | all-gather | bytes 442368 | tf_op jit(solution)/shard_map/all_gather | solution.py:75
  682.0 62.6 %all-reduce.3.cloned.1.call-done = (f32[512,512]{0,1:T(8,128)}, f32[256,256]{1,0:T(8,128)}, f32[256,256]{1,0:T(8,128)}, f32[512,512]{0,1:T(8,128)}) async-done(((f32[512,512]{0,1:T(8,128)}, f32[256,256]{1,0:T(8,128)}, f32[256,256]{1,0:T(8,128)}, f32[512,512]{0,1:T(8,128)}), (f32[512,512]{0,1:T(8,128)}, f32[256,256]{1,0:T(8,128)}, f32[256,256]{1,0:T(8,128)}, ...) | async-done | bytes 2621456 | tf_op jit(solution)/shard_map/psum | solution.py:88
  750.8 12.8 %copy.101 = bf16[48,8,32,512]{3,2,1,0:T(8,128)(2,1)} copy(bf16[48,8,32,512]{3,1,2,0:T(8,128)(2,1)} %bitcast.26) | data formatting | bytes 25165824
  763.6 65.3 %multiply_convert_fusion = bf16[384,32,512]{2,0,1:T(8,128)(2,1)} fusion(f32[384,32,512]{2,0,1:T(8,128)} %copy.82, bf16[384,32,512]{2,1,0:T(8,128)(2,1)} %bitcast.81, bf16[512,512]{1,0:T(8,128)(2,1)S(1)} %copy-done.5), kind=kOutput, calls=%fused_computation.5 | convolution fusion | flops 6455033856 | bytes 50855936 | tf_op jit(solution)/shard_map/cij,jk->cik/dot_general | solution.py:77
  828.9 16.7 %copy.83 = bf16[384,32,512]{0,2,1:T(8,128)(2,1)} copy(bf16[384,32,512]{2,0,1:T(8,128)(2,1)} %multiply_convert_fusion) | data formatting | bytes 25165824 | tf_op jit(solution)/shard_map/convert_element_type | solution.py:85
  845.6 16.6 %copy.88 = bf16[384,16384]{1,0:T(8,128)(2,1)} copy(bf16[384,16384]{0,1:T(8,128)(2,1)} %bitcast.83) | data formatting | bytes 25165824
  862.2 10.5 %copy.111 = bf16[384,16384]{1,0:T(8,128)(2,1)} copy(bf16[384,16384]{1,0:T(8,128)(2,1)} %bitcast.9) | data formatting | bytes 25165824
  (35 shorter events, 48.6 us)
Async XLA Ops:
  7.2 160.1 %copy-start = (f32[384,512]{1,0:T(8,128)S(1)}, f32[384,512]{1,0:T(8,128)}, u32[]{:S(2)}) copy-start(f32[384,512]{1,0:T(8,128)} %param.16) | copy-start | bytes 2359300
  161.1 144.4 %all-to-all-start.2 = ((bf16[8,48,16384]{2,1,0:T(8,128)(2,1)}), bf16[8,48,16384]{2,1,0:T(8,128)(2,1)}, u32[]{:S(2)}, u32[]{:S(2)}) async-start(bf16[8,48,16384]{2,1,0:T(8,128)(2,1)} %bitcast.85), calls=%async_computation.2 | async-start | bytes 25165824 | tf_op jit(solution)/shard_map/all_to_all | solution.py:31
  181.7 19.5 %copy-start.4 = (bf16[512,512]{1,0:T(8,128)(2,1)S(1)}, bf16[512,512]{1,0:T(8,128)(2,1)}, u32[]{:S(2)}) copy-start(bf16[512,512]{1,0:T(8,128)(2,1)} %param.15) | copy-start | bytes 1572868
  201.3 16.1 %copy-start.7 = (bf16[256,256]{1,0:T(8,128)(2,1)S(1)}, bf16[256,256]{1,0:T(8,128)(2,1)}, u32[]{:S(2)}) copy-start(bf16[256,256]{1,0:T(8,128)(2,1)} %param.14) | copy-start | bytes 393220
  212.8 4.5 copy-start.2
  217.4 10.1 %copy-start.6 = (bf16[256,256]{1,0:T(8,128)(2,1)S(1)}, bf16[256,256]{1,0:T(8,128)(2,1)}, u32[]{:S(2)}) copy-start(bf16[256,256]{1,0:T(8,128)(2,1)} %param.13) | copy-start | bytes 393220
  227.5 14.8 %copy-start.3 = (bf16[512,512]{1,0:T(8,128)(2,1)S(1)}, bf16[512,512]{1,0:T(8,128)(2,1)}, u32[]{:S(2)}) copy-start(bf16[512,512]{1,0:T(8,128)(2,1)} %param.12) | copy-start | bytes 1572868
  305.4 209.5 %all-to-all-start.1 = ((bf16[48,8,16384]{2,0,1:T(8,128)(2,1)}), bf16[48,8,16384]{2,0,1:T(8,128)(2,1)}, u32[]{:S(2)}, u32[]{:S(2)}) async-start(bf16[48,8,16384]{2,0,1:T(8,128)(2,1)} %copy.75), calls=%async_computation.1 | async-start | bytes 25165824 | tf_op jit(solution)/shard_map/all_to_all | solution.py:66
  514.9 235.9 %all-to-all-start.3 = ((bf16[48,8,16384]{2,0,1:T(8,128)(2,1)}), bf16[48,8,16384]{2,0,1:T(8,128)(2,1)}, u32[]{:S(2)}, u32[]{:S(2)}) async-start(bf16[48,8,16384]{2,0,1:T(8,128)(2,1)} %copy.80), calls=%async_computation.3 | async-start | bytes 25165824 | tf_op jit(solution)/shard_map/all_to_all | solution.py:69
  520.3 224.3 %all-reduce.3.cloned.1.call-start = ((), (), s32[]{:S(2)}) async-start(), calls=%async_computation.4 | async-start | bytes 5242880 | tf_op jit(solution)/shard_map/psum | solution.py:88
  564.6 106.4 %copy-start.8 = (f32[48,512]{1,0:T(8,128)S(1)}, f32[48,512]{1,0:T(8,128)}, u32[]{:S(2)}) copy-start(f32[48,512]{1,0:T(8,128)} %get-tuple-element.44) | copy-start | bytes 294916
  750.8 12.8 %copy-start.5 = (bf16[512,512]{1,0:T(8,128)(2,1)S(1)}, bf16[512,512]{1,0:T(8,128)(2,1)}, u32[]{:S(2)}) copy-start(bf16[512,512]{1,0:T(8,128)(2,1)} %param.15) | copy-start | bytes 1572868
  862.2 10.5 %copy-start.1 = (f32[384,512]{1,0:T(8,128)S(1)}, f32[384,512]{1,0:T(8,128)}, u32[]{:S(2)}) copy-start(f32[384,512]{1,0:T(8,128)} %param.16) | copy-start | bytes 2359300
Sparse Core Ops, SparseCore 0:
  564.7 179.7 all-reduce.2
where the time goes:
time: 894 us; the launch traced here: 880 us
  local copies, waits for them, and re-layouts  271 us (30%)
  blocking collectives  243 us (27%)
  matrix products  226 us (25%)
  waiting for transfers between devices  77.1 us (9%)
  other arithmetic  31.9 us (4%)
  starting transfers between devices  16.1 us (2%)
  between operations  14.5 us (2%)
    all_to_all x1, blocking collectives, local(): lax.all_to_all(up_gate, 'seq', split_axis=0, concat_axis=1, tiled=True)  144 us
    all_gather x1, blocking collectives, local(): lax.all_gather(rows_part, 'seq', axis=0, tiled=True)  89.7 us
    dot_general x1, matrix products, local(): jnp.einsum('cij,jk->cik', second_rows.reshape(width, rows_local, P2), fac...  65.3 us
    psum x1, waiting for transfers between devices, local(): lax.psum((grad_one, grad_two, grad_three, grad_four), ('seq', 'ch'))  62.6 us
    unnamed x23, local copies, waits for them, and re-layouts  47.1 us
    all_to_all x2, local copies, waits for them, and re-layouts, local(): lax.all_to_all(second.reshape(several, P1 * P2), 'seq', split_axis=1, con...  45.5 us
    all_to_all x2, local copies, waits for them, and re-layouts, local(): lax.all_to_all(local_input.reshape(several, P1 * P2), 'seq', split_axis=1...  34.3 us
    convert_element_type x1, local copies, waits for them, and re-layouts, local(): upstream.reshape(width, rows_local, P2).astype(flt) * final_prod  24.6 us
  transfers between devices with their start and end apart: 4, of which 2 were waited for; matrix products, arithmetic and copies ran while one was open for 40% of the time, Pallas kernels for 0%

commit v1 on v0

--- a/solution.py
+++ b/solution.py
@@ -66,8 +66,16 @@
         lax.all_to_all(
             local_input.reshape(several, P1 * P2), "seq", split_axis=1, concat_axis=0, tiled=True
         ),
-        lax.all_to_all(
-            second.reshape(several, P1 * P2), "seq", split_axis=1, concat_axis=0, tiled=True
+        jnp.concatenate(
+            lax.all_to_all(
+                jnp.stack(
+                    jnp.split(second.reshape(several, P1 * P2), lax.axis_size("seq"), axis=1)
+                ),
+                "seq",
+                0,
+                0,
+            ),
+            axis=0,
         ),
     )
     cols_sum, rows_sum = (

time: 894 us -> 944 us (1.056)
  waiting for transfers between devices: 77.1 us -> 287 us
  blocking collectives: 243 us -> 98.8 us
  local copies, waits for them, and re-layouts: 271 us -> 247 us
    all_to_all x1 -> x0, blocking collectives: 144 us -> none  [local(): lax.all_to_all(up_gate, 'seq', split_axis=0, concat_axis=1, tiled=True)]
    all_to_all x1, waiting for transfers between devices: 14.5 us -> 126 us  [local(): lax.all_to_all(inputs, 'seq', split_axis=0, concat_axis=1, tiled=True)]
    all_to_all x1 -> x2, waiting for transfers between devices: 0.01 us -> 61.9 us  [the longest x1 61.9 us: local(): lax.all_to_all(up_gate, 'seq', split_axis=0, concat_axis=1, tiled=True)]
    all_to_all x2 -> x0, local copies, waits for them, and re-layouts: 45.5 us -> none  [local(): lax.all_to_all(second.reshape(several, P1 * P2), 'seq', split_axis=1, con...]
    all_to_all x1, waiting for transfers between devices: 0.01 us -> 35.7 us  [local(): lax.all_to_all(local_input.reshape(several, P1 * P2), 'seq', split_axis=1...]
    unnamed x23 -> x31, local copies, waits for them, and re-layouts: 47.1 us -> 82.2 us
    convert_element_type x1 -> x0, local copies, waits for them, and re-layouts: 16.7 us -> none  [local(): jnp.einsum('ki,cij->ckj', factor_three, left_out, preferred_element_type=...]
  transfers between devices with their start and end apart: 4 -> 5, of which waited for: 2 -> 4; matrix products, arithmetic and copies ran while one was open for 40% -> 28% of each run, Pallas kernels for 0% -> 0%
where the time goes in v1:
time: 944 us; the launch traced here: 930 us
  waiting for transfers between devices  287 us (30%)
  local copies, waits for them, and re-layouts  247 us (26%)
  matrix products  226 us (24%)
  blocking collectives  98.8 us (10%)
  other arithmetic  35.8 us (4%)
  starting transfers between devices  21.5 us (2%)
  between operations  14.5 us (2%)
    all_to_all x1, waiting for transfers between devices, local(): lax.all_to_all(inputs, 'seq', split_axis=0, concat_axis=1, tiled=True)  126 us
    all_gather x1, blocking collectives, local(): lax.all_gather(rows_part, 'seq', axis=0, tiled=True)  89.5 us
    unnamed x31, local copies, waits for them, and re-layouts  82.2 us
    dot_general x1, matrix products, local(): jnp.einsum('cij,jk->cik', second_rows.reshape(width, rows_local, P2), fac...  65.3 us
    psum x1, waiting for transfers between devices, local(): lax.psum((grad_one, grad_two, grad_three, grad_four), ('seq', 'ch'))  63.3 us
    all_to_all x1, waiting for transfers between devices, local(): lax.all_to_all(up_gate, 'seq', split_axis=0, concat_axis=1, tiled=True)  61.9 us
    all_to_all x1, waiting for transfers between devices, local(): lax.all_to_all(local_input.reshape(several, P1 * P2), 'seq', split_axis=1...  35.7 us
    all_to_all x2, local copies, waits for them, and re-layouts, local(): lax.all_to_all(local_input.reshape(several, P1 * P2), 'seq', split_axis=1...  34.1 us
  transfers between devices with their start and end apart: 5, of which 4 were waited for; matrix products, arithmetic and copies ran while one was open for 28% of the time, Pallas kernels for 0%

profile of v1, /device:TPU:0, one launch (start us, length us, event | category | flops | bytes accessed | tf_op | source)
XLA Modules:
  0.0 930.5 jit_solution(7112915644549785530)
XLA Ops:
  12.7 13.8 %multiply_convert_fusion.4 = bf16[384,16384]{1,0:T(8,128)(2,1)} fusion(bf16[384,16384]{1,0:T(8,128)(2,1)} %param.10, bf16[384,16384]{1,0:T(8,128)(2,1)} %param.11), kind=kLoop, calls=%fused_computation.9 | loop fusion | flops 25165824 | bytes 37748736 | tf_op jit(solution)/shard_map/convert_element_type | solution.py:29
  26.5 125.9 %all-to-all-done.2 = bf16[8,48,16384]{2,1,0:T(8,128)(2,1)} async-done(((bf16[8,48,16384]{2,1,0:T(8,128)(2,1)}), bf16[8,48,16384]{2,1,0:T(8,128)(2,1)}, u32[]{:S(2)}, u32[]{:S(2)}) %all-to-all-start.2) | async-done | bytes 12582944 | tf_op jit(solution)/shard_map/all_to_all | solution.py:31
  157.7 17.6 %copy.74 = f32[384,16384]{0,1:T(8,128)} copy(bf16[384,16384]{1,0:T(8,128)(2,1)} %param.11) | data formatting | bytes 37748736 | tf_op jit(solution)/shard_map/convert_element_type | solution.py:29
  175.3 24.7 %copy.79 = f32[384,32,512]{2,0,1:T(8,128)} copy(f32[384,32,512]{0,2,1:T(8,128)} %bitcast.115) | data formatting | bytes 50331648 | tf_op jit(solution)/shard_map/convert_element_type | solution.py:92
  200.8 14.4 %copy.75 = bf16[48,8,16384]{2,1,0:T(8,128)(2,1)} copy(bf16[48,8,16384]{2,0,1:T(8,128)(2,1)} %bitcast.12) | data formatting | bytes 25165824 | tf_op jit(solution)/shard_map/all_to_all | solution.py:31
  215.3 19.6 %reshape.47 = bf16[48,256,512]{2,1,0:T(8,128)(2,1)} reshape(bf16[48,8,16384]{2,1,0:T(8,128)(2,1)} %copy.75) | data formatting | bytes 25165824 | tf_op jit(solution)/shard_map/reshape | solution.py:38
  234.8 61.9 %all-to-all-done = bf16[8,48,16384]{2,1,0:T(8,128)(2,1)} async-done(((bf16[8,48,16384]{2,1,0:T(8,128)(2,1)}), bf16[8,48,16384]{2,1,0:T(8,128)(2,1)}, u32[]{:S(2)}, u32[]{:S(2)}) %all-to-all-start) | async-done | bytes 12582944 | tf_op jit(solution)/shard_map/all_to_all | solution.py:32
  296.7 14.4 %copy.69 = bf16[48,8,16384]{2,1,0:T(8,128)(2,1)} copy(bf16[48,8,16384]{2,0,1:T(8,128)(2,1)} %bitcast.1) | data formatting | bytes 25165824 | tf_op jit(solution)/shard_map/all_to_all | solution.py:32
  311.1 19.5 %reshape.46 = bf16[48,256,512]{2,1,0:T(8,128)(2,1)} reshape(bf16[48,8,16384]{2,1,0:T(8,128)(2,1)} %copy.69) | data formatting | bytes 25165824 | tf_op jit(solution)/shard_map/reshape | solution.py:39
  330.7 11.6 %convolution_convert_fusion.1 = bf16[48,256,512]{2,1,0:T(8,128)(2,1)S(1)} fusion(bf16[48,256,512]{2,1,0:T(8,128)(2,1)} %reshape.46, bf16[512,512]{1,0:T(8,128)(2,1)S(1)} %copy-done.4), kind=kOutput, calls=%fused_computation.19 | convolution fusion | flops 6448742400 | bytes 25690112 | tf_op jit(solution)/shard_map/cik,jk->cij/dot_general | solution.py:48
  346.8 10.1 %fusion.47 = f32[48,512,256]{2,1,0:T(8,128)} fusion(bf16[48,256,512]{2,1,0:T(8,128)(2,1)S(1)} %convolution_convert_fusion.1, bf16[256,256]{1,0:T(8,128)(2,1)S(1)} %copy-done.7), kind=kOutput, calls=%fused_computation.55 | convolution fusion | flops 3221225472 | bytes 37879808 | tf_op jit(solution)/shard_map/ki,ckj->cij/dot_general | solution.py:52
  356.9 14.8 %convolution_convert_fusion = bf16[48,512,256]{1,2,0:T(8,128)(2,1)} fusion(f32[48,512,256]{2,1,0:T(8,128)} %fusion.47, f32[48,256]{1,0:T(8,128)S(1)} %constant_dynamic-slice_fusion.1, bf16[256,256]{1,0:T(8,128)(2,1)S(1)} %copy-done.6), kind=kOutput, calls=%fused_computation.17 | convolution fusion | flops 3240099840 | bytes 37928960 | tf_op jit(solution)/shard_map/ki,ckj->cij/dot_general | solution.py:56
  371.7 14.6 %fusion.10 = bf16[48,256,512]{2,1,0:T(8,128)(2,1)} fusion(bf16[48,512,256]{1,2,0:T(8,128)(2,1)} %convolution_convert_fusion, f32[48,512]{1,0:T(8,128)S(1)} %constant_dynamic-slice_fusion, bf16[512,512]{1,0:T(8,128)(2,1)S(1)} %copy-done.3), kind=kOutput, calls=%fused_computation.18 | convolution fusion | flops 6467616768 | bytes 25788416 | tf_op jit(solution)/shard_map/cik,jk->cij/dot_general | solution.py:62
  386.3 19.6 %all_to_all.44 = bf16[48,8,16384]{2,1,0:T(8,128)(2,1)} reshape(bf16[48,256,512]{2,1,0:T(8,128)(2,1)} %fusion.10) | data formatting | bytes 25165824 | tf_op jit(solution)/shard_map/all_to_all | solution.py:66
  405.9 14.5 %copy.73 = bf16[48,8,16384]{2,0,1:T(8,128)(2,1)} copy(bf16[48,8,16384]{2,1,0:T(8,128)(2,1)} %all_to_all.44) | data formatting | bytes 25165824 | tf_op jit(solution)/shard_map/all_to_all | solution.py:66
  425.7 18.9 %fusion.1 = (f32[48,512]{1,0:T(8,128)}, f32[48,256,512]{2,1,0:T(8,128)}) fusion(bf16[48,512,256]{1,2,0:T(8,128)(2,1)} %convolution_convert_fusion, bf16[48,256,512]{2,1,0:T(8,128)(2,1)} %reshape.47, bf16[512,512]{1,0:T(8,128)(2,1)S(1)} %copy-done.3), kind=kOutput, calls=%fused_computation.3 | convolution fusion | flops 6461300736 | bytes 50954240 | tf_op jit(solution)/shard_map/cij,jk->cik/dot_general | solution.py:40
  444.6 16.3 %fusion.21 = f32[48,512,256]{2,1,0:T(8,128)} fusion(f32[48,256,512]{2,1,0:T(8,128)} %get-tuple-element.45, f32[48,512]{1,0:T(8,128)S(1)} %constant_dynamic-slice_fusion, bf16[256,256]{1,0:T(8,128)(2,1)S(1)} %copy-done.6), kind=kOutput, calls=%fused_computation.22 | convolution fusion | flops 3233808384 | bytes 50561024 | tf_op jit(solution)/shard_map/ki,cij->ckj/dot_general | solution.py:42
  460.9 14.4 %convert_bitcast_fusion = bf16[48,256,512]{1,2,0:T(8,128)(2,1)} fusion(f32[48,512,256]{2,1,0:T(8,128)} %fusion.21, f32[48,256]{1,0:T(8,128)S(1)} %constant_dynamic-slice_fusion.1, bf16[256,256]{1,0:T(8,128)(2,1)S(1)} %copy-done.7), kind=kOutput, calls=%fused_computation.14 | convolution fusion | flops 3240099840 | bytes 37928960 | tf_op jit(solution)/shard_map/ki,cij->ckj/dot_general | solution.py:44
  475.3 16.4 %copy.98 = bf16[6,8,256,512]{3,1,2,0:T(8,128)(2,1)} copy(bf16[6,8,256,512]{2,3,1,0:T(8,128)(2,1)} %bitcast.114) | data formatting | bytes 25165824
  505.1 15.8 %fusion.36 = f32[256,256]{1,0:T(8,128)} fusion(bf16[48,256,512]{2,1,0:T(8,128)(2,1)} %copy-done.2, f32[48,512,256]{2,1,0:T(8,128)} %fusion.21, f32[48,256]{1,0:T(8,128)S(1)} %constant_dynamic-slice_fusion.1), kind=kOutput, calls=%fused_computation.42 | convolution fusion | flops 3233808384 | bytes 38060032 | tf_op jit(solution)/shard_map/ckj,cij->ki/dot_general | solution.py:51
  529.0 35.7 %all-to-all-done.1 = bf16[48,8,16384]{2,0,1:T(8,128)(2,1)} async-done(((bf16[48,8,16384]{2,0,1:T(8,128)(2,1)}), bf16[48,8,16384]{2,0,1:T(8,128)(2,1)}, u32[]{:S(2)}, u32[]{:S(2)}) %all-to-all-start.1) | async-done | bytes 12582944 | tf_op jit(solution)/shard_map/all_to_all | solution.py:66
  570.1 14.3 %fusion.30 = f32[512,512]{0,1:T(8,128)} fusion(bf16[48,256,512]{2,1,0:T(8,128)(2,1)} %reshape.47, bf16[48,512,256]{1,2,0:T(8,128)(2,1)} %convolution_convert_fusion, f32[48,512]{1,0:T(8,128)S(1)} %constant_dynamic-slice_fusion), kind=kOutput, calls=%fused_computation.39 | convolution fusion | flops 6461325312 | bytes 26312704 | tf_op jit(solution)/shard_map/cij,cik->jk/dot_general | solution.py:61
  584.4 12.6 %convolution_bitcast_fusion = f32[512,512]{0,1:T(8,128)} fusion(bf16[48,256,512]{1,2,0:T(8,128)(2,1)} %convert_bitcast_fusion, bf16[48,256,512]{2,1,0:T(8,128)(2,1)} %reshape.46), kind=kOutput, calls=%fused_computation.40 | convolution fusion | flops 6442450944 | bytes 26214400 | tf_op jit(solution)/shard_map/cij,cik->jk/dot_general | solution.py:47
  597.0 17.6 %fusion.33 = f32[256,256]{1,0:T(8,128)} fusion(f32[48,256,512]{2,1,0:T(8,128)} %get-tuple-element.45, f32[48,512]{1,0:T(8,128)S(1)} %constant_dynamic-slice_fusion, f32[48,512,256]{2,1,0:T(8,128)} %fusion.47, f32[48,256]{1,0:T(8,128)S(1)} %constant_dynamic-slice_fusion.1), kind=kOutput, calls=%fused_computation.41 | convolution fusion | flops 3246391296 | bytes 50741248 | tf_op jit(solution)/shard_map/ckj,cij->ki/dot_general | solution.py:55
  614.6 16.6 %multiply_reduce_fusion = f32[48,256]{1,0:T(8,128)S(1)} fusion(f32[48,512,256]{2,1,0:T(8,128)} %fusion.47, f32[48,512,256]{2,1,0:T(8,128)} %fusion.21), kind=kLoop, calls=%fused_computation.4 | loop fusion | flops 12570624 | bytes 50380800 | tf_op jit(solution)/shard_map/reduce_sum | solution.py:53
  631.3 89.5 %all_gather.7 = f32[384,256]{1,0:T(8,128)S(1)} all-gather(f32[48,256]{1,0:T(8,128)S(1)} %multiply_reduce_fusion), channel_id=1, replica_groups=mesh['seq'=8,'ch'=4] {'seq'}, dimensions={0}, use_global_device_ids=true | all-gather | bytes 442368 | tf_op jit(solution)/shard_map/all_gather | solution.py:83
  731.8 63.3 %all-reduce.3.cloned.1.call-done = (f32[512,512]{0,1:T(8,128)}, f32[256,256]{1,0:T(8,128)}, f32[256,256]{1,0:T(8,128)}, f32[512,512]{0,1:T(8,128)}) async-done(((f32[512,512]{0,1:T(8,128)}, f32[256,256]{1,0:T(8,128)}, f32[256,256]{1,0:T(8,128)}, f32[512,512]{0,1:T(8,128)}), (f32[512,512]{0,1:T(8,128)}, f32[256,256]{1,0:T(8,128)}, f32[256,256]{1,0:T(8,128)}, ...) | async-done | bytes 2621456 | tf_op jit(solution)/shard_map/psum | solution.py:96
  801.4 12.8 %copy.99 = bf16[48,8,32,512]{3,2,1,0:T(8,128)(2,1)} copy(bf16[48,8,32,512]{3,1,2,0:T(8,128)(2,1)} %bitcast.35) | data formatting | bytes 25165824
  814.2 65.3 %multiply_convert_fusion = bf16[384,32,512]{2,0,1:T(8,128)(2,1)} fusion(f32[384,32,512]{2,0,1:T(8,128)} %copy.79, bf16[384,32,512]{2,1,0:T(8,128)(2,1)} %bitcast.116, bf16[512,512]{1,0:T(8,128)(2,1)S(1)} %copy-done.5), kind=kOutput, calls=%fused_computation.5 | convolution fusion | flops 6455033856 | bytes 50855936 | tf_op jit(solution)/shard_map/cij,jk->cik/dot_general | solution.py:85
  879.5 16.6 %copy.80 = bf16[384,32,512]{0,2,1:T(8,128)(2,1)} copy(bf16[384,32,512]{2,0,1:T(8,128)(2,1)} %multiply_convert_fusion) | data formatting | bytes 25165824 | tf_op jit(solution)/shard_map/convert_element_type | solution.py:93
  896.1 16.6 %copy.85 = bf16[384,16384]{1,0:T(8,128)(2,1)} copy(bf16[384,16384]{0,1:T(8,128)(2,1)} %bitcast.125) | data formatting | bytes 25165824
  912.7 10.5 %copy.117 = bf16[384,16384]{1,0:T(8,128)(2,1)} copy(bf16[384,16384]{1,0:T(8,128)(2,1)} %bitcast.9) | data formatting | bytes 25165824
  (42 shorter events, 65.5 us)
Async XLA Ops:
  7.2 193.7 %copy-start = (f32[384,512]{1,0:T(8,128)S(1)}, f32[384,512]{1,0:T(8,128)}, u32[]{:S(2)}) copy-start(f32[384,512]{1,0:T(8,128)} %param.16) | copy-start | bytes 2359300
  7.2 145.2 %all-to-all-start.2 = ((bf16[8,48,16384]{2,1,0:T(8,128)(2,1)}), bf16[8,48,16384]{2,1,0:T(8,128)(2,1)}, u32[]{:S(2)}, u32[]{:S(2)}) async-start(bf16[8,48,16384]{2,1,0:T(8,128)(2,1)} %bitcast.127), calls=%async_computation.2 | async-start | bytes 25165824 | tf_op jit(solution)/shard_map/all_to_all | solution.py:31
  152.4 144.3 %all-to-all-start = ((bf16[8,48,16384]{2,1,0:T(8,128)(2,1)}), bf16[8,48,16384]{2,1,0:T(8,128)(2,1)}, u32[]{:S(2)}, u32[]{:S(2)}) async-start(bf16[8,48,16384]{2,1,0:T(8,128)(2,1)} %bitcast.126), calls=%async_computation | async-start | bytes 25165824 | tf_op jit(solution)/shard_map/all_to_all | solution.py:32
  311.1 19.5 %copy-start.4 = (bf16[512,512]{1,0:T(8,128)(2,1)S(1)}, bf16[512,512]{1,0:T(8,128)(2,1)}, u32[]{:S(2)}) copy-start(bf16[512,512]{1,0:T(8,128)(2,1)} %param.15) | copy-start | bytes 1572868
  330.7 16.1 %copy-start.7 = (bf16[256,256]{1,0:T(8,128)(2,1)S(1)}, bf16[256,256]{1,0:T(8,128)(2,1)}, u32[]{:S(2)}) copy-start(bf16[256,256]{1,0:T(8,128)(2,1)} %param.14) | copy-start | bytes 393220
  342.3 4.5 copy-start.2
  346.8 10.1 %copy-start.6 = (bf16[256,256]{1,0:T(8,128)(2,1)S(1)}, bf16[256,256]{1,0:T(8,128)(2,1)}, u32[]{:S(2)}) copy-start(bf16[256,256]{1,0:T(8,128)(2,1)} %param.13) | copy-start | bytes 393220
  356.9 14.8 %copy-start.3 = (bf16[512,512]{1,0:T(8,128)(2,1)S(1)}, bf16[512,512]{1,0:T(8,128)(2,1)}, u32[]{:S(2)}) copy-start(bf16[512,512]{1,0:T(8,128)(2,1)} %param.12) | copy-start | bytes 1572868
  420.4 144.3 %all-to-all-start.1 = ((bf16[48,8,16384]{2,0,1:T(8,128)(2,1)}), bf16[48,8,16384]{2,0,1:T(8,128)(2,1)}, u32[]{:S(2)}, u32[]{:S(2)}) async-start(bf16[48,8,16384]{2,0,1:T(8,128)(2,1)} %copy.73), calls=%async_computation.1 | async-start | bytes 25165824 | tf_op jit(solution)/shard_map/all_to_all | solution.py:66
  564.7 236.7 %all-to-all-start.3 = ((bf16[8,48,16384]{2,1,0:T(8,128)(2,1)}), bf16[8,48,16384]{2,1,0:T(8,128)(2,1)}, u32[]{:S(2)}, u32[]{:S(2)}) async-start(bf16[8,48,16384]{2,1,0:T(8,128)(2,1)} %fusion.22), calls=%async_computation.3 | async-start | bytes 25165824 | tf_op jit(solution)/shard_map/all_to_all | solution.py:70
  570.1 225.0 %all-reduce.3.cloned.1.call-start = ((), (), s32[]{:S(2)}) async-start(), calls=%async_computation.4 | async-start | bytes 5242880 | tf_op jit(solution)/shard_map/psum | solution.py:96
  614.6 106.2 %copy-start.8 = (f32[48,512]{1,0:T(8,128)S(1)}, f32[48,512]{1,0:T(8,128)}, u32[]{:S(2)}) copy-start(f32[48,512]{1,0:T(8,128)} %get-tuple-element.44) | copy-start | bytes 294916
  801.4 12.8 %copy-start.5 = (bf16[512,512]{1,0:T(8,128)(2,1)S(1)}, bf16[512,512]{1,0:T(8,128)(2,1)}, u32[]{:S(2)}) copy-start(bf16[512,512]{1,0:T(8,128)(2,1)} %param.15) | copy-start | bytes 1572868
  912.7 10.5 %copy-start.1 = (f32[384,512]{1,0:T(8,128)S(1)}, f32[384,512]{1,0:T(8,128)}, u32[]{:S(2)}) copy-start(f32[384,512]{1,0:T(8,128)} %param.16) | copy-start | bytes 2359300
Sparse Core Ops, SparseCore 0:
  614.7 180.2 all-reduce.2
